TPU v7x, 32 devices: a whole 2x2x4 slice. The times are simulated.
32 devices in a mesh: dp: 2 (over y), seq: 4 (over z), chan: 4 (over x, core).
Axes of the slice: x: 2, y: 2, z: 4, core: 2. Of those that a mesh axis runs over, the one named last changes fastest.
Arguments:
- tokens: bfloat16 [16384, 1024], P(('dp', 'seq'), 'chan'), may hold values from -6 to 6
- gain_one: bfloat16 [1024], P('chan'), may hold values from 0.25 to 1.75
- in_weight: bfloat16 [1024, 3, 1024], P(None, None, 'chan'), may hold values from -0.1875 to 0.1875
- conv_weight: bfloat16 [3, 1024], P(None, 'chan'), may hold values from -3 to 3
- out_weight: bfloat16 [1024, 1024], P('chan'), may hold values from -0.1875 to 0.1875
- gain_two: bfloat16 [1024], replicated, may hold values from 0.25 to 1.75
- gate_up_weight: bfloat16 [1024, 2, 4608], P(None, None, 'chan'), may hold values from -0.1875 to 0.1875
- down_weight: bfloat16 [4608, 1024], P('chan'), may hold values from -0.09375 to 0.09375
- cotangent: bfloat16 [16384, 1024], P(('dp', 'seq'), 'chan'), may hold values from -6 to 6
Outputs:
- result: bfloat16 [16384, 1024], P(('dp', 'seq'), 'chan')
- grad_tokens: bfloat16 [16384, 1024], P(('dp', 'seq'), 'chan')
- grad_gain_one: float32 [1024], P('chan')
- grad_in_weight: float32 [1024, 3, 1024], P(None, None, 'chan')
- grad_conv_weight: float32 [3, 1024], P(None, 'chan')
- grad_out_weight: float32 [1024, 1024], P('chan')
- grad_gain_two: float32 [1024], P('chan')
- grad_gate_up: float32 [1024, 2, 4608], P(None, None, 'chan')
- grad_down: float32 [4608, 1024], P('chan')
All inputs are finite; a program needn't handle non-finite values.
Results may differ from a plain program's by a relative error of at most 0.018.
Values may be sent and summed in bfloat16 or wider, within the bound.
No kernel may reach another device: no remote copies, remote signals or barrier semaphores. Data moves between devices by JAX's collectives and lax.ppermute only.
A program may use at most 256 MiB of HBM per device.

v0:
```python
import jax
import jax.numpy as jnp
from jax import lax
from jax.sharding import PartitionSpec as P

epsilon = 1e-05


def shifted(value, axis, by):
    length = lax.axis_size(axis)
    pairs = [(i, i + by) for i in range(length) if 0 <= i + by < length]
    return lax.ppermute(value, axis, pairs)


def shards(
    tokens,
    gain_one,
    in_weight,
    conv_weight,
    out_weight,
    gain_two,
    gate_up_weight,
    down_weight,
    cotangent,
):
    width = in_weight.shape[0]
    local_width = in_weight.shape[2]
    hidden_local = gate_up_weight.shape[2]
    count = tokens.shape[0]
    offset = lax.axis_index("chan") * local_width
    in_flat = in_weight.reshape(width, 3 * local_width)
    gu_flat = gate_up_weight.reshape(width, 2 * hidden_local)
    kernel = conv_weight.astype(jnp.float32)
    gain_second = gain_two.astype(jnp.float32)
    tokens_local = tokens.astype(jnp.float32)
    tokens_full, gain_full = (
        lax.all_gather(tokens, "chan", axis=1, tiled=True),
        lax.all_gather(gain_one, "chan", axis=0, tiled=True),
    )
    x_float = tokens_full.astype(jnp.float32)
    inv_one = lax.rsqrt(jnp.mean(x_float * x_float, axis=-1, keepdims=True) + epsilon)
    normed_one = (x_float * inv_one * gain_full.astype(jnp.float32)).astype(jnp.bfloat16)
    projected = jnp.dot(normed_one, in_flat, preferred_element_type=jnp.float32)
    gate_b = projected[:, :local_width]
    gate_c = projected[:, local_width : 2 * local_width]
    values = projected[:, 2 * local_width :]
    product = gate_b * values
    state = shifted(product[count - 2 :], "seq", 1)
    extended = jnp.concatenate([state, product], axis=0)
    conv_out = (
        kernel[0] * extended[0:count]
        + kernel[1] * extended[1 : count + 1]
        + kernel[2] * extended[2 : count + 2]
    )
    mixed = (gate_c * conv_out).astype(jnp.bfloat16)
    mix_partial = jnp.dot(mixed, out_weight, preferred_element_type=jnp.float32)
    resid = x_float + lax.psum(mix_partial, "chan")
    inv_two = lax.rsqrt(jnp.mean(resid * resid, axis=-1, keepdims=True) + epsilon)
    scaled_two = resid * inv_two
    normed_two = (scaled_two * gain_second).astype(jnp.bfloat16)
    resid_local = lax.dynamic_slice_in_dim(resid, offset, local_width, 1)
    gate_up = jnp.dot(normed_two, gu_flat, preferred_element_type=jnp.float32)
    gate_pre = gate_up[:, :hidden_local]
    up_pre = gate_up[:, hidden_local:]
    sigma = jax.nn.sigmoid(gate_pre)
    hidden = (gate_pre * sigma * up_pre).astype(jnp.bfloat16)
    ffn_local = lax.psum_scatter(
        jnp.dot(hidden, down_weight, preferred_element_type=jnp.float32).astype(jnp.bfloat16),
        "chan",
        scatter_dimension=1,
        tiled=True,
    ).astype(jnp.float32)
    result = (resid_local + ffn_local).astype(jnp.bfloat16)
    cot_full = lax.all_gather(cotangent, "chan", axis=1, tiled=True)
    d_hidden = jnp.dot(cot_full, down_weight.T, preferred_element_type=jnp.float32)
    grad_down = jnp.dot(hidden.T, cot_full, preferred_element_type=jnp.float32)
    d_gate = d_hidden * up_pre * sigma * (1.0 + gate_pre * (1.0 - sigma))
    d_up = d_hidden * gate_pre * sigma
    d_gate_up = jnp.concatenate([d_gate, d_up], axis=1).astype(jnp.bfloat16)
    grad_gate_up = jnp.dot(normed_two.T, d_gate_up, preferred_element_type=jnp.float32).reshape(
        width, 2, hidden_local
    )
    norm_partial = jnp.dot(d_gate_up, gu_flat.T, preferred_element_type=jnp.float32)
    d_norm_two = lax.psum(norm_partial, "chan")
    grad_gain_two = lax.dynamic_slice_in_dim(
        jnp.sum(d_norm_two * scaled_two, axis=0), offset, local_width, 0
    )
    pulled_two = d_norm_two * gain_second
    d_resid = cot_full.astype(jnp.float32) + inv_two * (
        pulled_two - scaled_two * jnp.mean(pulled_two * scaled_two, axis=-1, keepdims=True)
    )
    d_out = d_resid.astype(jnp.bfloat16)
    d_resid_local = lax.dynamic_slice_in_dim(d_resid, offset, local_width, 1)
    d_mixed = jnp.dot(d_out, out_weight.T, preferred_element_type=jnp.float32)
    grad_out = jnp.dot(mixed.T, d_out, preferred_element_type=jnp.float32)
    d_gate_c = d_mixed * conv_out
    d_conv = d_mixed * gate_c
    next_grad = shifted(d_conv[0:2], "seq", -1)
    grad_ext = jnp.concatenate([d_conv, next_grad], axis=0)
    d_product = (
        kernel[2] * grad_ext[0:count]
        + kernel[1] * grad_ext[1 : count + 1]
        + kernel[0] * grad_ext[2 : count + 2]
    )
    grad_conv = jnp.stack(
        [
            jnp.sum(d_conv * extended[shift_index : shift_index + count], axis=0)
            for shift_index in range(3)
        ]
    )
    d_project = jnp.concatenate([d_product * values, d_gate_c, d_product * gate_b], axis=1).astype(
        jnp.bfloat16
    )
    grad_in = jnp.dot(normed_one.T, d_project, preferred_element_type=jnp.float32).reshape(
        width, 3, local_width
    )
    d_norm_one = lax.psum_scatter(
        jnp.dot(d_project, in_flat.T, preferred_element_type=jnp.float32).astype(jnp.bfloat16),
        "chan",
        scatter_dimension=1,
        tiled=True,
    ).astype(jnp.float32)
    scaled_one = tokens_local * inv_one
    grad_gain_one = jnp.sum(d_norm_one * scaled_one, axis=0)
    pulled_one = d_norm_one * gain_one.astype(jnp.float32)
    inner_sum = lax.psum(jnp.sum(pulled_one * scaled_one, axis=-1, keepdims=True), "chan")
    grad_tokens = (
        d_resid_local + inv_one * (pulled_one - scaled_one * (inner_sum / width))
    ).astype(jnp.bfloat16)
    grad_gain_one, grad_in, grad_conv, grad_out, grad_gain_two, grad_gate_up, grad_down = (
        lax.psum(grad_gain_one.astype(jnp.bfloat16), ("dp", "seq")).astype(jnp.float32),
        lax.psum(grad_in.astype(jnp.bfloat16), ("dp", "seq")).astype(jnp.float32),
        lax.psum(grad_conv.astype(jnp.bfloat16), ("dp", "seq")).astype(jnp.float32),
        lax.psum(grad_out.astype(jnp.bfloat16), ("dp", "seq")).astype(jnp.float32),
        lax.psum(grad_gain_two.astype(jnp.bfloat16), ("dp", "seq")).astype(jnp.float32),
        lax.psum(grad_gate_up.astype(jnp.bfloat16), ("dp", "seq")).astype(jnp.float32),
        lax.psum(grad_down.astype(jnp.bfloat16), ("dp", "seq")).astype(jnp.float32),
    )
    return (
        result,
        grad_tokens,
        grad_gain_one,
        grad_in,
        grad_conv,
        grad_out,
        grad_gain_two,
        grad_gate_up,
        grad_down,
    )


def solution(mesh):
    placed = (
        P(("dp", "seq"), "chan"),
        P("chan"),
        P(None, None, "chan"),
        P(None, "chan"),
        P("chan", None),
        P(),
        P(None, None, "chan"),
        P("chan", None),
        P(("dp", "seq"), "chan"),
    )
    return jax.shard_map(
        shards,
        mesh=mesh,
        in_specs=placed,
        out_specs=(
            P(("dp", "seq"), "chan"),
            P(("dp", "seq"), "chan"),
            P("chan"),
            P(None, None, "chan"),
            P(None, "chan"),
            P("chan", None),
            P("chan"),
            P(None, None, "chan"),
            P("chan", None),
        ),
        check_vma=False,
    )
```

profile of v0, /device:TPU:0, one launch (start us, length us, event | category | flops | bytes accessed | tf_op | source)
XLA Modules:
  0.0 858.1 jit_solution(401732263966881372)
XLA Ops:
  8.0 2.6 copy.25
  10.6 6.0 all-gather
  16.6 30.7 %all-gather.4.cloned.1.call-done = bf16[2048,1024]{1,0:T(8,128)(2,1)} async-done(((bf16[2048,256]{1,0:T(8,128)(2,1)}), bf16[2048,1024]{1,0:T(8,128)(2,1)}) %all-gather.4.cloned.1.call-update) | async-done | bytes 4194320 | tf_op jit(solution)/shard_map/all_gather | solution.py:37
  47.3 3.2 fusion
  50.8 5.0 fusion.27
  56.1 3.5 collective-permute-start
  59.7 1.3 collective-permute-done
  61.0 2.0 multiply_convert_fusion.7
  63.0 1.0 copy-done.10
  64.0 4.7 fusion.36
  69.8 5.4 copy.30
  75.1 147.3 %all-reduce.6.cloned.1.call-done = f32[2048,1024]{1,0:T(8,128)} async-done(((f32[2048,1024]{1,0:T(8,128)}), f32[2048,1024]{1,0:T(8,128)}) %all-reduce.6.cloned.1.call-update) | async-done | bytes 8388624 | tf_op jit(solution)/shard_map/psum | solution.py:57
  222.5 5.7 multiply_reduce_fusion.2
  228.2 3.4 copy-done.3
  231.6 16.3 %fusion.33 = f32[2048,2304]{1,0:T(8,128)} fusion(bf16[1024,2304]{1,0:T(8,128)(2,1)} %bitcast.27, f32[2048,1024]{1,0:T(8,128)S(1)} %get-tuple-element.27, f32[1024]{0:T(1024)S(1)} %convert_element_type.107, f32[2048]{0:T(1024)S(1)} %add_rsqrt_fusion), kind=kOutput, calls=%fused_computation.73 | convolution fusion | flops 9669967872 | bytes 31993856 | tf_op jit(solution)/shard_map/dot_general | solution.py:62
  247.9 11.3 %all-gather.6.cloned.1.call-done = bf16[2048,1024]{1,0:T(8,128)(2,1)} async-done(((bf16[2048,256]{1,0:T(8,128)(2,1)}), bf16[2048,1024]{1,0:T(8,128)(2,1)}) %all-gather.6.cloned.1.call-update) | async-done | bytes 4194320 | tf_op jit(solution)/shard_map/all_gather | solution.py:74
  259.2 18.2 %multiply_convert_fusion.1 = (bf16[2048,1152]{1,0:T(8,128)(2,1)}, bf16[2048,1152]{1,0:T(8,128)(2,1)}, bf16[2048,1152]{1,0:T(8,128)(2,1)}) fusion(f32[2048,2304]{1,0:T(8,128)} %fusion.33, bf16[2048,1024]{1,0:T(8,128)(2,1)} %all-gather.6.cloned.1.call-done, bf16[1152,1024]{1,0:T(8,128)(2,1)S(1)} %copy-done), kind=kOutput, calls=%fused_computation.5 | convolution fusion | flops 4869586944 | bytes 39583744 | tf_op jit(solution)/shard_map/dot_general | solution.py:75
  277.4 15.8 %fusion.4 = f32[2048,1024]{1,0:T(8,128)} fusion(bf16[1024,2304]{1,0:T(8,128)(2,1)} %bitcast.28, bf16[2048,1152]{1,0:T(8,128)(2,1)} %get-tuple-element.31, bf16[2048,1152]{1,0:T(8,128)(2,1)} %get-tuple-element.30), kind=kOutput, calls=%fused_computation.17 | convolution fusion | flops 9682550784 | bytes 22544384 | tf_op jit(solution)/shard_map/dot_general | solution.py:83
  293.9 9.5 %convolution_convert_fusion.1 = bf16[2048,1024]{1,0:T(8,128)(2,1)} fusion(bf16[2048,1152]{1,0:T(8,128)(2,1)} %get-tuple-element.32, bf16[1152,1024]{1,0:T(8,128)(2,1)S(1)} %copy-done), kind=kOutput, calls=%fused_computation.20 | convolution fusion | flops 4833935360 | bytes 11272192 | tf_op jit(solution)/shard_map/dot_general | solution.py:68
  303.5 142.9 %all-reduce.8.cloned.1.call-done = f32[2048,1024]{1,0:T(8,128)} async-done(((f32[2048,1024]{1,0:T(8,128)}), f32[2048,1024]{1,0:T(8,128)}) %all-reduce.8.cloned.1.call-update) | async-done | bytes 8388624 | tf_op jit(solution)/shard_map/psum | solution.py:84
  446.3 7.1 multiply_reduce_fusion
  453.4 1.4 copy-done.4
  454.9 7.7 multiply_add_fusion
  462.6 2.9 fusion.21
  465.5 1.4 copy-done.2
  466.9 1.4 copy-done.13
  468.2 1.1 multiply_reduce_fusion.5
  469.4 1.3 collective-permute-start.1
  470.7 4.2 collective-permute-done.1
  477.0 0.9 copy-done.16
  477.8 5.0 convolution_convert_fusion.2
  483.0 16.9 %fusion.5 = bf16[1024,2304]{1,0:T(8,128)(2,1)} fusion(bf16[2048,1152]{1,0:T(8,128)(2,1)} %get-tuple-element.31, bf16[2048,1152]{1,0:T(8,128)(2,1)} %get-tuple-element.30, f32[2048,1024]{1,0:T(8,128)} %copy-done.3, f32[1024]{0:T(1024)S(1)} %convert_element_type.107, f32[2048]{0:T(1024)S(1)} %add_rsqrt_fusion), kind=kOutput, calls=%fused_computation.18 | convolution fusion | flops 9691201536 | bytes 22556672 | tf_op jit(solution)/shard_map/dot_general | solution.py:80
  500.0 10.3 %convert_element_type.131 = bf16[1024,2,1152]{2,1,0:T(2,128)(2,1)} reshape(bf16[1024,2304]{1,0:T(8,128)(2,1)} %fusion.5) | data formatting | bytes 9437184 | tf_op jit(solution)/shard_map/convert_element_type | solution.py:136
  510.3 9.6 %convolution_convert_fusion = bf16[1152,1024]{1,0:T(8,128)(2,1)} fusion(bf16[2048,1152]{1,0:T(8,128)(2,1)} %get-tuple-element.32, bf16[2048,1024]{1,0:T(8,128)(2,1)} %all-gather.6.cloned.1.call-done), kind=kOutput, calls=%fused_computation.19 | convolution fusion | flops 4833017856 | bytes 11272192 | tf_op jit(solution)/shard_map/dot_general | solution.py:76
  519.9 5.6 fusion.23
  525.6 4.0 convolution_convert_fusion.3
  529.6 1.6 copy.28
  531.9 3.2 add_convert_fusion
  535.1 5.0 reduce-scatter.5.cloned.1.call-done
  540.1 2.1 fusion.17
  542.2 22.3 %all-reduce = (bf16[256]{0:T(256)(128)(2,1)S(1)}, bf16[3,256]{1,0:T(4,128)(2,1)S(1)}, bf16[256]{0:T(256)(128)(2,1)S(1)}) all-reduce(bf16[256]{0:T(256)(128)(2,1)S(1)} %get-tuple-element.14, bf16[3,256]{1,0:T(4,128)(2,1)S(1)} %pad_maximum_fusion.10, ...), channel_id=1, replica_groups=mesh['dp'=2,'seq'=4,'chan'=4] {'dp','seq'}, use_global_device_ids=true, to_apply=%region_10.0 | all-reduce | flops 1280 | bytes 5120 | tf_op jit(solution)/shard_map/psum | solution.py:131
  566.3 6.1 psum.72
  572.4 3.1 fusion.16
  575.6 262.1 %all-reduce.10.cloned.1.call-done = (bf16[1024,3,256]{2,0,1:T(8,128)(2,1)}, bf16[256,1024]{1,0:T(8,128)(2,1)}, bf16[1024,2,1152]{2,1,0:T(2,128)(2,1)}, bf16[1152,1024]{1,0:T(8,128)(2,1)}) async-done(((bf16[1024,3,256]{2,0,1:T(8,128)(2,1)}, bf16[256,1024]{1,0:T(8,128)(2,1)}, bf16[1024,2,1152]{2,1,0:T(2,128)(2,1)}, bf16[1152,1024]{1,0:T(8,128)(2,1)}), (bf16[1024,3,256]{2,0,1:T(8,128)(2,1)}, ...) | async-done | bytes 9175056 | tf_op jit(solution)/shard_map/psum | solution.py:132
  837.7 7.3 convert_element_type.132
  845.0 2.9 convert_element_type.134
  848.0 1.9 convert_element_type.124
  849.9 1.1 convert_element_type.127
  (98 shorter events, 8.0 us)
Async XLA Ops:
  7.2 252.0 %copy-start = (bf16[1152,1024]{1,0:T(8,128)(2,1)S(1)}, bf16[1152,1024]{1,0:T(8,128)(2,1)}, u32[]{:S(2)}) copy-start(bf16[1152,1024]{1,0:T(8,128)(2,1)} %param.16) | copy-start | bytes 7077892
  7.2 3.4 copy-start.29
  7.2 40.1 %all-gather.4.cloned.1.call-start = ((), (), s32[]{:S(2)}) async-start(), calls=%async_computation.2 | async-start | bytes 5242880 | tf_op jit(solution)/shard_map/all_gather | solution.py:37
  7.9 214.5 %all-reduce.6.cloned.1.call-start = ((), (), s32[]{:S(2)}) async-start(), calls=%async_computation.3 | async-start | bytes 16777216 | tf_op jit(solution)/shard_map/psum | solution.py:57
  16.6 39.2 %copy-start.26 = (f32[4,1,256]{2,1,0:T(1,128)}, f32[4,1,256]{2,1,0:T(1,128)S(1)}, u32[]{:S(2)}) copy-start(f32[4,1,256]{2,1,0:T(1,128)S(1)} %convert_element_type.135) | copy-start | bytes 12292
  47.3 3.4 copy-start.8
  50.6 5.2 copy-start.23
  55.8 7.2 copy-start.5
  55.8 3.9 copy-start.25
  56.1 6.9 copy-start.6
  56.1 7.9 copy-start.15
  56.1 4.8 collective-permute-start
  63.0 1.0 copy-start.10
  68.6 1.1 copy-start.28
  68.7 190.5 %all-gather.6.cloned.1.call-start = ((), (), s32[]{:S(2)}) async-start(), calls=%async_computation.5 | async-start | bytes 5242880 | tf_op jit(solution)/shard_map/all_gather | solution.py:74
  69.4 376.9 %all-reduce.8.cloned.1.call-start = ((), (), s32[]{:S(2)}) async-start(), calls=%async_computation.6 | async-start | bytes 16777216 | tf_op jit(solution)/shard_map/psum | solution.py:84
  228.2 3.4 copy-start.3
  293.3 238.6 %reduce-scatter.3.cloned.1.call-start = ((), (), s32[]{:S(2)}) async-start(), calls=%async_computation.4 | async-start | bytes 5242880 | tf_op jit(solution)/shard_map/reduce_scatter | solution.py:67
  303.4 236.7 %reduce-scatter.5.cloned.1.call-start = ((), (), s32[]{:S(2)}) async-start(), calls=%async_computation.7 | async-start | bytes 5242880 | tf_op jit(solution)/shard_map/reduce_scatter | solution.py:117
  446.3 8.5 copy-start.4
  446.3 20.5 %slice-start = ((s8[6291456]{0:T(1024)(128)(4,1)}), s8[4194304]{0:T(1024)(128)(4,1)S(1)}, s32[]{:S(2)}) async-start(s8[6291456]{0:T(1024)(128)(4,1)} %bitcast.24), calls=%async_computation.9 | async-start | bytes 8388608
  454.9 12.0 %slice-start.1 = ((s8[6291456]{0:T(1024)(128)(4,1)}), s8[2097152]{0:T(1024)(128)(4,1)S(1)}, s32[]{:S(2)}) async-start(s8[6291456]{0:T(1024)(128)(4,1)} %bitcast.24), calls=%async_computation.10 | async-start | bytes 4194304
  462.6 4.3 copy-start.2
  462.6 4.3 copy-start.7
  462.6 5.6 copy-start.13
  469.4 5.5 collective-permute-start.1
  475.6 1.0 copy-start.18
  475.6 2.2 copy-start.16
  476.0 1.0 copy-start.20
  482.8 354.9 %all-reduce.10.cloned.1.call-start = ((), (), s32[]{:S(2)}) async-start(), calls=%async_computation.8 | async-start | bytes 18350080 | tf_op jit(solution)/shard_map/psum | solution.py:132
  510.3 9.6 %copy-start.11 = (bf16[2048,256]{1,0:T(8,128)(2,1)S(1)}, bf16[2048,256]{1,0:T(8,128)(2,1)}, u32[]{:S(2)}) copy-start(bf16[2048,256]{1,0:T(8,128)(2,1)} %copy-done.10) | copy-start | bytes 3145732
  519.8 5.7 copy-start.9
  519.9 5.7 copy-start.19
  519.9 5.7 copy-start.21
  519.9 5.7 copy-start.24
  519.9 5.7 copy-start.27
  531.1 0.7 copy-start.30
  531.8 8.3 copy-start.12
  837.7 7.3 copy-start.14
  845.0 3.0 copy-start.17
  845.0 4.9 copy-start.22
  845.0 6.0 copy-start.1
Sparse Core Ops, SparseCore 0:
  9.6 37.7 all-gather.3
  68.8 153.6 all-reduce.5
  224.0 35.1 all-gather.5
  293.4 152.8 all-reduce.7
  448.7 44.5 reduce-scatter.2
  495.7 44.3 reduce-scatter.4
  545.9 291.7 all-reduce.9
where the time goes:
time: 864 us; the launch traced here: 858 us
  waiting for transfers between devices  606 us (70%)
  matrix products  114 us (13%)
  other arithmetic  51.8 us (6%)
  blocking collectives  34.5 us (4%)
  local copies, waits for them, and re-layouts  31.2 us (4%)
  between operations  14.8 us (2%)
    psum x1, waiting for transfers between devices, shards(): lax.psum(grad_in.astype(jnp.bfloat16), ('dp', 'seq')).astype(jnp.float32)  262 us
    psum x1, waiting for transfers between devices, shards(): resid = x_float + lax.psum(mix_partial, 'chan')  147 us
    psum x1, waiting for transfers between devices, shards(): d_norm_two = lax.psum(norm_partial, 'chan')  143 us
    all_gather x1, waiting for transfers between devices, shards(): lax.all_gather(tokens, 'chan', axis=1, tiled=True)  30.7 us
    psum x1, blocking collectives, shards(): lax.psum(grad_gain_one.astype(jnp.bfloat16), ('dp', 'seq'))  22.3 us
    unnamed x69, local copies, waits for them, and re-layouts  19.2 us
    dot_general x1, matrix products, shards(): jnp.dot(cot_full, down_weight.T, preferred_element_type=jnp.float32)  18.2 us
  transfers between devices with their start and end apart: 9, of which 8 were waited for; matrix products, arithmetic and copies ran while one was open for 14% of the time, Pallas kernels for 0%

commit v1 on v0

--- a/solution.py
+++ b/solution.py
@@ -1,9 +1,18 @@
+import functools
 import jax
 import jax.numpy as jnp
 from jax import lax
 from jax.sharding import PartitionSpec as P
+from jax.lax import all_gather
 
 epsilon = 1e-05
+
+
+def test_results_here(page, mesh_dim):
+    return jnp.sum(all_gather(page, mesh_dim), axis=0)
+
+
+expand_orders = functools.partial(test_results_here, mesh_dim="chan")
 
 
 def shifted(value, axis, by):
@@ -54,7 +63,7 @@
     )
     mixed = (gate_c * conv_out).astype(jnp.bfloat16)
     mix_partial = jnp.dot(mixed, out_weight, preferred_element_type=jnp.float32)
-    resid = x_float + lax.psum(mix_partial, "chan")
+    resid = x_float + expand_orders(mix_partial)
     inv_two = lax.rsqrt(jnp.mean(resid * resid, axis=-1, keepdims=True) + epsilon)
     scaled_two = resid * inv_two
     normed_two = (scaled_two * gain_second).astype(jnp.bfloat16)

time: 864 us -> 919 us (1.064)
  waiting for transfers between devices: 606 us -> 644 us
  other arithmetic: 51.8 us -> 68.9 us
    all_gather x0 -> x1, waiting for transfers between devices: none -> 196 us  [test_results_here(): return jnp.sum(all_gather(page, mesh_dim), axis=0)]
    psum x1 -> x0, waiting for transfers between devices: 147 us -> none  [shards(): resid = x_float + lax.psum(mix_partial, 'chan')]
    reduce_sum x0 -> x1, other arithmetic: none -> 17.2 us  [test_results_here(): return jnp.sum(all_gather(page, mesh_dim), axis=0)]
    all_gather x1, waiting for transfers between devices: 11.3 us -> 0.01 us  [shards(): cot_full = lax.all_gather(cotangent, 'chan', axis=1, tiled=True)]
    unnamed x69 -> x73, local copies, waits for them, and re-layouts: 19.2 us -> 19.3 us
  transfers between devices with their start and end apart: 9 -> 9, of which waited for: 8 -> 7; matrix products, arithmetic and copies ran while one was open for 14% -> 15% of each run, Pallas kernels for 0% -> 0%
where the time goes in v1:
time: 919 us; the launch traced here: 912 us
  waiting for transfers between devices  644 us (70%)
  matrix products  113 us (12%)
  other arithmetic  68.9 us (7%)
  blocking collectives  34.5 us (4%)
  local copies, waits for them, and re-layouts  31.2 us (3%)
  between operations  14.9 us (2%)
    psum x1, waiting for transfers between devices, shards(): lax.psum(grad_in.astype(jnp.bfloat16), ('dp', 'seq')).astype(jnp.float32)  262 us
    all_gather x1, waiting for transfers between devices, test_results_here(): return jnp.sum(all_gather(page, mesh_dim), axis=0)  196 us
    psum x1, waiting for transfers between devices, shards(): d_norm_two = lax.psum(norm_partial, 'chan')  143 us
    all_gather x1, waiting for transfers between devices, shards(): lax.all_gather(tokens, 'chan', axis=1, tiled=True)  30.7 us
    psum x1, blocking collectives, shards(): lax.psum(grad_gain_one.astype(jnp.bfloat16), ('dp', 'seq'))  22.3 us
    unnamed x73, local copies, waits for them, and re-layouts  19.3 us
  transfers between devices with their start and end apart: 9, of which 7 were waited for; matrix products, arithmetic and copies ran while one was open for 15% of the time, Pallas kernels for 0%

profile of v1, /device:TPU:0, one launch (start us, length us, event | category | flops | bytes accessed | tf_op | source)
XLA Modules:
  0.0 912.2 jit_solution(16951768124615259269)
XLA Ops:
  8.0 2.6 copy.25
  10.6 6.0 all-gather.1
  16.6 30.7 %all-gather.6.cloned.1.call-done = bf16[2048,1024]{1,0:T(8,128)(2,1)} async-done(((bf16[2048,256]{1,0:T(8,128)(2,1)}), bf16[2048,1024]{1,0:T(8,128)(2,1)}) %all-gather.6.cloned.1.call-update) | async-done | bytes 4194320 | tf_op jit(solution)/shard_map/all_gather | solution.py:46
  47.3 3.2 fusion
  50.8 5.0 fusion.27
  56.1 3.5 collective-permute-start
  59.7 1.3 collective-permute-done
  61.0 2.0 multiply_convert_fusion.7
  63.0 1.0 copy-done.10
  64.0 4.7 fusion.36
  70.0 5.4 copy.30
  75.4 195.8 %all-gather.10.cloned.1.call-done = f32[8192,1024]{1,0:T(8,128)} async-done(((f32[2048,1024]{1,0:T(8,128)}), f32[8192,1024]{1,0:T(8,128)}) %all-gather.10.cloned.1.call-update) | async-done | bytes 33554448 | tf_op jit(solution)/shard_map/all_gather | solution.py:12
  271.2 17.2 %reduce_sum.91 = f32[2048,1024]{1,0:T(8,128)} reduce(f32[4,2048,1024]{2,1,0:T(8,128)} %bitcast.25, f32[]{:T(128)} %constant.8.clone.1), dimensions={0}, to_apply=%region_1.0 | reduce | flops 6291456 | bytes 41943044 | tf_op jit(solution)/shard_map/reduce_sum | solution.py:12
  288.4 5.7 multiply_reduce_fusion.2
  294.2 3.4 copy-done.3
  297.5 15.7 %fusion.33 = f32[2048,2304]{1,0:T(8,128)} fusion(bf16[1024,2304]{1,0:T(8,128)(2,1)} %bitcast.29, f32[2048,1024]{1,0:T(8,128)S(1)} %get-tuple-element.27, f32[1024]{0:T(1024)S(1)} %convert_element_type.107, f32[2048]{0:T(1024)S(1)} %add_rsqrt_fusion), kind=kOutput, calls=%fused_computation.73 | convolution fusion | flops 9669967872 | bytes 31993856 | tf_op jit(solution)/shard_map/dot_general | solution.py:71
  313.3 18.2 %multiply_convert_fusion.1 = (bf16[2048,1152]{1,0:T(8,128)(2,1)}, bf16[2048,1152]{1,0:T(8,128)(2,1)}, bf16[2048,1152]{1,0:T(8,128)(2,1)}) fusion(f32[2048,2304]{1,0:T(8,128)} %fusion.33, bf16[2048,1024]{1,0:T(8,128)(2,1)} %all-gather.8.cloned.1.call-done, bf16[1152,1024]{1,0:T(8,128)(2,1)S(1)} %copy-done), kind=kOutput, calls=%fused_computation.5 | convolution fusion | flops 4869586944 | bytes 39583744 | tf_op jit(solution)/shard_map/dot_general | solution.py:84
  331.5 15.9 %fusion.4 = f32[2048,1024]{1,0:T(8,128)} fusion(bf16[1024,2304]{1,0:T(8,128)(2,1)} %bitcast.30, bf16[2048,1152]{1,0:T(8,128)(2,1)} %get-tuple-element.31, bf16[2048,1152]{1,0:T(8,128)(2,1)} %get-tuple-element.30), kind=kOutput, calls=%fused_computation.17 | convolution fusion | flops 9682550784 | bytes 22544384 | tf_op jit(solution)/shard_map/dot_general | solution.py:92
  347.6 9.5 %convolution_convert_fusion.1 = bf16[2048,1024]{1,0:T(8,128)(2,1)} fusion(bf16[2048,1152]{1,0:T(8,128)(2,1)} %get-tuple-element.32, bf16[1152,1024]{1,0:T(8,128)(2,1)S(1)} %copy-done), kind=kOutput, calls=%fused_computation.20 | convolution fusion | flops 4833935360 | bytes 11272192 | tf_op jit(solution)/shard_map/dot_general | solution.py:77
  357.2 143.3 %all-reduce.5.cloned.1.call-done = f32[2048,1024]{1,0:T(8,128)} async-done(((f32[2048,1024]{1,0:T(8,128)}), f32[2048,1024]{1,0:T(8,128)}) %all-reduce.5.cloned.1.call-update) | async-done | bytes 8388624 | tf_op jit(solution)/shard_map/psum | solution.py:93
  500.5 7.1 multiply_reduce_fusion
  507.6 1.4 copy-done.4
  509.0 7.7 multiply_add_fusion
  516.7 2.9 fusion.21
  519.6 1.4 copy-done.2
  521.0 1.4 copy-done.13
  522.4 1.1 multiply_reduce_fusion.5
  523.4 1.3 collective-permute-start.1
  524.7 4.2 collective-permute-done.1
  531.1 0.9 copy-done.16
  531.9 4.9 convolution_convert_fusion.2
  537.1 16.9 %fusion.5 = bf16[1024,2304]{1,0:T(8,128)(2,1)} fusion(bf16[2048,1152]{1,0:T(8,128)(2,1)} %get-tuple-element.31, bf16[2048,1152]{1,0:T(8,128)(2,1)} %get-tuple-element.30, f32[2048,1024]{1,0:T(8,128)} %copy-done.3, f32[1024]{0:T(1024)S(1)} %convert_element_type.107, f32[2048]{0:T(1024)S(1)} %add_rsqrt_fusion), kind=kOutput, calls=%fused_computation.18 | convolution fusion | flops 9691201536 | bytes 22556672 | tf_op jit(solution)/shard_map/dot_general | solution.py:89
  554.1 10.3 %convert_element_type.131 = bf16[1024,2,1152]{2,1,0:T(2,128)(2,1)} reshape(bf16[1024,2304]{1,0:T(8,128)(2,1)} %fusion.5) | data formatting | bytes 9437184 | tf_op jit(solution)/shard_map/convert_element_type | solution.py:145
  564.4 9.6 %convolution_convert_fusion = bf16[1152,1024]{1,0:T(8,128)(2,1)} fusion(bf16[2048,1152]{1,0:T(8,128)(2,1)} %get-tuple-element.32, bf16[2048,1024]{1,0:T(8,128)(2,1)} %all-gather.8.cloned.1.call-done), kind=kOutput, calls=%fused_computation.19 | convolution fusion | flops 4833017856 | bytes 11272192 | tf_op jit(solution)/shard_map/dot_general | solution.py:85
  574.1 5.6 fusion.23
  579.7 4.0 convolution_convert_fusion.3
  583.7 1.6 copy.28
  586.1 3.2 add_convert_fusion
  589.3 5.0 reduce-scatter.5.cloned.1.call-done
  594.3 2.1 fusion.17
  596.4 22.3 %all-reduce = (bf16[256]{0:T(256)(128)(2,1)S(1)}, bf16[3,256]{1,0:T(4,128)(2,1)S(1)}, bf16[256]{0:T(256)(128)(2,1)S(1)}) all-reduce(bf16[256]{0:T(256)(128)(2,1)S(1)} %get-tuple-element.14, bf16[3,256]{1,0:T(4,128)(2,1)S(1)} %pad_maximum_fusion.10, ...), channel_id=1, replica_groups=mesh['dp'=2,'seq'=4,'chan'=4] {'dp','seq'}, use_global_device_ids=true, to_apply=%region_10.0 | all-reduce | flops 1280 | bytes 5120 | tf_op jit(solution)/shard_map/psum | solution.py:140
  620.4 6.1 psum.64
  626.6 3.1 fusion.16
  629.7 262.1 %all-reduce.7.cloned.1.call-done = (bf16[1024,3,256]{2,0,1:T(8,128)(2,1)}, bf16[256,1024]{1,0:T(8,128)(2,1)}, bf16[1024,2,1152]{2,1,0:T(2,128)(2,1)}, bf16[1152,1024]{1,0:T(8,128)(2,1)}) async-done(((bf16[1024,3,256]{2,0,1:T(8,128)(2,1)}, bf16[256,1024]{1,0:T(8,128)(2,1)}, bf16[1024,2,1152]{2,1,0:T(2,128)(2,1)}, bf16[1152,1024]{1,0:T(8,128)(2,1)}), (bf16[1024,3,256]{2,0,1:T(8,128)(2,1)}, ...) | async-done | bytes 9175056 | tf_op jit(solution)/shard_map/psum | solution.py:141
  891.9 7.3 convert_element_type.132
  899.2 2.9 convert_element_type.134
  902.1 1.9 convert_element_type.124
  904.0 1.1 convert_element_type.127
  (103 shorter events, 7.9 us)
Async XLA Ops:
  7.2 306.1 %copy-start = (bf16[1152,1024]{1,0:T(8,128)(2,1)S(1)}, bf16[1152,1024]{1,0:T(8,128)(2,1)}, u32[]{:S(2)}) copy-start(bf16[1152,1024]{1,0:T(8,128)(2,1)} %param.16) | copy-start | bytes 7077892
  7.2 3.4 copy-start.31
  7.2 40.1 %all-gather.6.cloned.1.call-start = ((), (), s32[]{:S(2)}) async-start(), calls=%async_computation.2 | async-start | bytes 5242880 | tf_op jit(solution)/shard_map/all_gather | solution.py:46
  7.9 263.2 %all-gather.10.cloned.1.call-start = ((), (), s32[]{:S(2)}) async-start(), calls=%async_computation.7 | async-start | bytes 41943040 | tf_op jit(solution)/shard_map/all_gather | solution.py:12
  16.6 39.2 %copy-start.28 = (f32[4,1,256]{2,1,0:T(1,128)}, f32[4,1,256]{2,1,0:T(1,128)S(1)}, u32[]{:S(2)}) copy-start(f32[4,1,256]{2,1,0:T(1,128)S(1)} %convert_element_type.135) | copy-start | bytes 12292
  47.3 3.4 copy-start.8
  50.6 5.2 copy-start.25
  55.8 7.2 copy-start.5
  55.8 3.9 copy-start.27
  56.1 6.9 copy-start.6
  56.1 7.9 copy-start.15
  56.1 4.8 collective-permute-start
  63.0 1.0 copy-start.10
  68.7 1.3 copy-start.30
  68.7 244.6 %all-gather.8.cloned.1.call-start = ((), (), s32[]{:S(2)}) async-start(), calls=%async_computation.4 | async-start | bytes 5242880 | tf_op jit(solution)/shard_map/all_gather | solution.py:83
  69.5 431.0 %all-reduce.5.cloned.1.call-start = ((), (), s32[]{:S(2)}) async-start(), calls=%async_computation.5 | async-start | bytes 16777216 | tf_op jit(solution)/shard_map/psum | solution.py:93
  294.1 3.4 copy-start.3
  347.4 238.7 %reduce-scatter.3.cloned.1.call-start = ((), (), s32[]{:S(2)}) async-start(), calls=%async_computation.3 | async-start | bytes 5242880 | tf_op jit(solution)/shard_map/reduce_scatter | solution.py:76
  357.2 237.1 %reduce-scatter.5.cloned.1.call-start = ((), (), s32[]{:S(2)}) async-start(), calls=%async_computation.6 | async-start | bytes 5242880 | tf_op jit(solution)/shard_map/reduce_scatter | solution.py:126
  500.5 8.5 copy-start.4
  500.5 20.5 %slice-start = ((s8[6291456]{0:T(1024)(128)(4,1)}), s8[4194304]{0:T(1024)(128)(4,1)S(1)}, s32[]{:S(2)}) async-start(s8[6291456]{0:T(1024)(128)(4,1)} %bitcast.26), calls=%async_computation.9 | async-start | bytes 8388608
  509.0 12.0 %slice-start.1 = ((s8[6291456]{0:T(1024)(128)(4,1)}), s8[2097152]{0:T(1024)(128)(4,1)S(1)}, s32[]{:S(2)}) async-start(s8[6291456]{0:T(1024)(128)(4,1)} %bitcast.26), calls=%async_computation.10 | async-start | bytes 4194304
  516.7 4.3 copy-start.2
  516.7 4.3 copy-start.7
  516.7 5.6 copy-start.13
  523.4 6.7 copy-start.18
  523.4 5.5 collective-permute-start.1
  529.7 1.0 copy-start.20
  529.7 2.2 copy-start.16
  530.1 1.0 copy-start.22
  536.9 355.0 %all-reduce.7.cloned.1.call-start = ((), (), s32[]{:S(2)}) async-start(), calls=%async_computation.8 | async-start | bytes 18350080 | tf_op jit(solution)/shard_map/psum | solution.py:141
  564.4 9.6 %copy-start.11 = (bf16[2048,256]{1,0:T(8,128)(2,1)S(1)}, bf16[2048,256]{1,0:T(8,128)(2,1)}, u32[]{:S(2)}) copy-start(bf16[2048,256]{1,0:T(8,128)(2,1)} %copy-done.10) | copy-start | bytes 3145732
  574.0 5.7 copy-start.9
  574.0 5.7 copy-start.19
  574.0 5.7 copy-start.21
  574.0 5.7 copy-start.23
  574.0 5.7 copy-start.26
  574.0 5.7 copy-start.29
  585.3 0.7 copy-start.32
  585.9 8.3 copy-start.12
  891.9 7.3 copy-start.14
  899.1 3.0 copy-start.17
  899.2 4.9 copy-start.24
  899.2 6.0 copy-start.1
Sparse Core Ops, SparseCore 0:
  9.6 37.7 all-gather.5
  68.8 202.2 all-gather.9
  272.7 34.9 all-gather.7
  347.5 152.9 all-reduce.4
  502.9 44.5 reduce-scatter.2
  549.8 44.3 reduce-scatter.4
  600.0 291.7 all-reduce.6
